TPU v7x, 512 devices: a whole 4x4x16 slice. The times are simulated.
512 devices in a mesh: ctx: 32 (over x, y, core), head: 16 (over z).
Axes of the slice: x: 4, y: 4, z: 16, core: 2. Of those that a mesh axis runs over, the one named last changes fastest.
Arguments:
- mixed_in: bfloat16 [8192, 8192], P(('ctx', 'head')), may hold values from -6 to 6
- conv_weight: float32 [4, 8192], P(None, 'head'), may hold values from -3 to 3
- write_strength_logit: float32 [32, 8192], P('head', 'ctx'), may hold values from -10.5 to 2.2, as said below
- decay_log: float32 [32, 8192], P('head', 'ctx'), may hold values from -0.7 to 0, as said below
- initial_state: float32 [32, 128, 128], P('head'), may hold values from -6 to 6
- final_state_grad: float32 [32, 128, 128], P('head'), may hold values from -6 to 6
- grad_out: bfloat16 [8192, 4096], P('ctx', 'head'), may hold values from -6 to 6
Outputs:
- grad_mixed: bfloat16 [8192, 8192], P(('ctx', 'head'))
- grad_conv: float32 [4, 8192], P(None, 'head')
- grad_beta_logit: float32 [32, 8192], P('head', 'ctx')
- grad_decay_log: float32 [32, 8192], P('head', 'ctx')
Inputs may be any that keep to these rules, and one draw needn't show every extreme that they name: `write_strength_logit`: each value head's write strengths and decays vary from token to token. `decay_log`: every entry is negative.
All inputs are finite; a program needn't handle non-finite values.
Results may differ from a plain program's by a relative error of at most 0.001.
Values may be sent and summed in bfloat16 or wider, within the bound.
A program may use at most 64 MiB of HBM per device.

v0:
```python
import jax
import jax.numpy as jnp
from jax import lax
from jax.sharding import PartitionSpec as P

HK = 16
VALUE_HEADS = 32
DK = 128
DV = 128
KW = 4
BLOCK = 64
highest = lax.Precision.HIGHEST
norm_eps = 1e-06


def from_behind(value, axis, by):
    devices = lax.axis_size(axis)
    pairs = [(i, i + by) for i in range(devices) if 0 <= i + by < devices]
    return lax.ppermute(value, axis, pairs)


def prefix(value, axis, combine, identity, reverse):
    devices, mine = (lax.axis_size(axis), lax.axis_index(axis))
    everything = jax.tree.map(lambda part: lax.all_gather(part, axis), value)
    start = jax.tree.map(
        lambda part, zero: jnp.broadcast_to(jnp.asarray(zero, part.dtype), part.shape),
        value,
        identity,
    )

    def step(k, before):
        at = devices - 1 - k if reverse else k
        reached = at > mine if reverse else at < mine
        new = combine(before, jax.tree.map(lambda part: part[at], everything))
        return jax.tree.map(lambda a, b: jnp.where(reached, a, b), new, before)

    return lax.fori_loop(0, devices, step, start)


def block_step(carried, pieces):
    state, transit = carried
    queries, key_feats, values, beta_gate, log_decay = pieces
    block_size = log_decay.shape[0]
    cumulative = jnp.cumsum(log_decay)
    row_ids = lax.broadcasted_iota(jnp.int32, (block_size, block_size), 0)
    col_ids = lax.broadcasted_iota(jnp.int32, (block_size, block_size), 1)
    causal = col_ids <= row_ids
    differ = jnp.where(causal, cumulative[:, None] - cumulative[None, :], 0.0)
    ratios = jnp.where(causal, jnp.exp(differ), 0.0)
    key_gram = jnp.dot(key_feats, key_feats.T, precision=highest)
    lower_part = jnp.where(col_ids < row_ids, beta_gate[:, None] * ratios * key_gram, 0.0)
    system = lower_part + jnp.eye(block_size, dtype=jnp.float32)
    decays = jnp.exp(cumulative)
    right_sides = jnp.concatenate(
        [beta_gate[:, None] * values, (beta_gate * decays)[:, None] * key_feats], axis=1
    )
    solved = jax.scipy.linalg.solve_triangular(system, right_sides, lower=True)
    width_v = values.shape[1]
    base_update = solved[:, :width_v]
    weights = solved[:, width_v:]
    update = base_update - jnp.dot(weights, state, precision=highest)
    scores = ratios * jnp.dot(queries, key_feats.T, precision=highest)
    output = decays[:, None] * jnp.dot(queries, state, precision=highest) + jnp.dot(
        scores, update, precision=highest
    )
    total_decay = jnp.exp(cumulative[-1])
    tail_keys = jnp.exp(cumulative[-1] - cumulative)[:, None] * key_feats
    new_state = total_decay * state + jnp.dot(tail_keys.T, update, precision=highest)
    step_map = total_decay * jnp.eye(key_feats.shape[1], dtype=jnp.float32) - jnp.dot(
        tail_keys.T, weights, precision=highest
    )
    new_transit = jnp.dot(step_map, transit, precision=highest)
    return ((new_state, new_transit), output)


def run_head(state, queries, key_feats, values, beta_gate, log_decay):
    blocks = queries.shape[0] // BLOCK
    pieces = (
        queries.reshape(blocks, BLOCK, -1),
        key_feats.reshape(blocks, BLOCK, -1),
        values.reshape(blocks, BLOCK, -1),
        beta_gate.reshape(blocks, BLOCK),
        log_decay.reshape(blocks, BLOCK),
    )
    start = (state, jnp.eye(key_feats.shape[1], dtype=jnp.float32))
    (state_end, transit), outputs = lax.scan(block_step, start, pieces)
    return (outputs.reshape(-1, values.shape[1]), state_end, transit)


def normalize(feats, factor):
    return feats * lax.rsqrt(jnp.sum(feats * feats, axis=-1, keepdims=True) + norm_eps) * factor


def mix_layer(state_in, extended, conv_weight, write_strength_logit, decay_log):
    row_count = extended.shape[0] - (KW - 1)
    filtered_signal = conv_weight[0] * extended[0:row_count]
    for tap in range(1, KW):
        filtered_signal = filtered_signal + conv_weight[tap] * extended[tap : tap + row_count]
    activated = jax.nn.silu(filtered_signal)
    ratio_heads = VALUE_HEADS // HK
    group_width = 2 * DK + ratio_heads * DV
    groups = activated.reshape(row_count, -1, group_width)
    key_heads = groups.shape[1]
    queries = normalize(groups[:, :, :DK], DK ** (-0.5))
    key_feats = normalize(groups[:, :, DK : 2 * DK], 1.0)
    values = (
        groups[:, :, 2 * DK :].reshape(row_count, key_heads * ratio_heads, DV).transpose(1, 0, 2)
    )
    queries = jnp.repeat(queries.transpose(1, 0, 2), ratio_heads, axis=0)
    key_feats = jnp.repeat(key_feats.transpose(1, 0, 2), ratio_heads, axis=0)
    beta_gate = jax.nn.sigmoid(write_strength_logit)
    outputs, state_out, transit = jax.vmap(run_head)(
        state_in, queries, key_feats, values, beta_gate, decay_log
    )
    result = outputs.transpose(1, 0, 2).reshape(row_count, -1)
    return ((result, state_out), transit)


def compose(earlier, later):
    matrix = jnp.einsum("hij,hjk->hik", later[0], earlier[0], precision=highest)
    offset = jnp.einsum("hij,hjk->hik", later[0], earlier[1], precision=highest) + later[1]
    return (matrix, offset)


def advance(maps, state):
    return jnp.einsum("hij,hjk->hik", maps[0], state, precision=highest) + maps[1]


def on_device(
    mixed_in,
    conv_weight,
    write_strength_logit,
    decay_log,
    initial_state,
    final_state_grad,
    grad_out,
):
    local_in = lax.all_to_all(mixed_in, "head", split_axis=1, concat_axis=0, tiled=True)
    edge_rows = from_behind(local_in[-(KW - 1) :], "ctx", 1)
    extended = jnp.concatenate([edge_rows, local_in], axis=0).astype(jnp.float32)
    cotangent = grad_out.astype(jnp.float32)
    zeros_state = jnp.zeros_like(initial_state)

    def from_state(state):
        return mix_layer(state, extended, conv_weight, write_strength_logit, decay_log)

    primal, pull_state, transit = jax.vjp(from_state, zeros_state, has_aux=True)
    offset = primal[1]
    local_grad = pull_state((cotangent, jnp.zeros_like(offset)))[0]
    flipped = jnp.swapaxes(transit, 1, 2)
    identity = (
        jnp.broadcast_to(jnp.eye(transit.shape[1], dtype=jnp.float32), transit.shape),
        jnp.zeros_like(offset),
    )
    earlier_map = prefix((transit, offset), "ctx", compose, identity, False)
    later_map = prefix((flipped, local_grad), "ctx", compose, identity, True)
    state_in = advance(earlier_map, initial_state)
    state_grad = advance(later_map, final_state_grad)

    def forward(ext_rows, weight_taps, logits, decay_logs):
        return mix_layer(state_in, ext_rows, weight_taps, logits, decay_logs)

    unused, pull_all, unused_transit = jax.vjp(
        forward, extended, conv_weight, write_strength_logit, decay_log, has_aux=True
    )
    grad_ext, grad_weight, grad_beta, grad_decay = pull_all((cotangent, state_grad))
    spilled = from_behind(grad_ext[: KW - 1], "ctx", -1)
    own_grad = grad_ext[KW - 1 :]
    own_grad = jnp.concatenate([own_grad[: -(KW - 1)], own_grad[-(KW - 1) :] + spilled], axis=0)
    returned = lax.all_to_all(
        own_grad.astype(jnp.bfloat16), "head", split_axis=0, concat_axis=1, tiled=True
    )
    weight_total = lax.psum(grad_weight, "ctx")
    return (returned, weight_total, grad_beta, grad_decay)


def solution(mesh):
    in_specs = (
        P(("ctx", "head"), None),
        P(None, "head"),
        P("head", "ctx"),
        P("head", "ctx"),
        P("head", None, None),
        P("head", None, None),
        P("ctx", "head"),
    )
    out_specs = (P(("ctx", "head"), None), P(None, "head"), P("head", "ctx"), P("head", "ctx"))
    return jax.shard_map(
        on_device, mesh=mesh, in_specs=in_specs, out_specs=out_specs, check_vma=False
    )
```

profile of v0, /device:TPU:32, one launch (start us, length us, event | category | flops | bytes accessed | tf_op | source)
XLA Modules:
  0.0 795.1 jit_solution(5155768118002871086)
XLA Ops:
  8.9 15.2 %all-to-all-start = ((bf16[16,16,512]{2,0,1:T(8,128)(2,1)}), bf16[16,16,512]{2,0,1:T(8,128)(2,1)S(1)}, u32[]{:S(2)}, u32[]{:S(2)}) async-start(bf16[16,16,512]{2,0,1:T(8,128)(2,1)} %bitcast.435), calls=%async_computation | async-start | bytes 524288 | tf_op jit(solution)/shard_map/all_to_all | solution.py:138
  26.4 15.6 %all-to-all-done = bf16[16,16,512]{2,0,1:T(8,128)(2,1)S(1)} async-done(((bf16[16,16,512]{2,0,1:T(8,128)(2,1)}), bf16[16,16,512]{2,0,1:T(8,128)(2,1)S(1)}, u32[]{:S(2)}, u32[]{:S(2)}) %all-to-all-start) | async-done | bytes 262176 | tf_op jit(solution)/shard_map/all_to_all | solution.py:138
  48.5 65.6 %while.169 = (s32[]{:T(128)}, f32[2,128,128]{2,1,0:T(8,128)S(1)}, f32[2,128,128]{2,1,0:T(8,128)S(1)}, f32[4,2,64,128]{3,2,1,0:T(8,128)S(1)}, f32[4,2,64,1]{2,1,3...) while((s32[]{:T(128)}, f32[2,128,128]{2,1,0:T(8,128)S(1)}, ...), condition=%wide.region_4.6_spmd.clone.clone, body=%wide.region_2.5_spmd.clone.clone.sunk | while | flops 176640128 | bytes 2980628 | solution.py:86
  51.5 9.8 %custom-call.35 = f32[2,1,64,64]{2,3,1,0:T(8,128)S(1)} custom-call(f32[2,1,64,64]{3,2,1,0:T(8,128)S(1)} %fusion.420), custom_call_target="InvertDiagBlocksLowerTriangular" | custom-call | tf_op jit(solution)/shard_map/jvp(vmap())/while/body/eval_jaxpr/jit(_solve_triangular)/triangular_solve/custom-call.1 | solution.py:57
  67.9 9.8 %custom-call.35 = f32[2,1,64,64]{2,3,1,0:T(8,128)S(1)} custom-call(f32[2,1,64,64]{3,2,1,0:T(8,128)S(1)} %fusion.420), custom_call_target="InvertDiagBlocksLowerTriangular" | custom-call | tf_op jit(solution)/shard_map/jvp(vmap())/while/body/eval_jaxpr/jit(_solve_triangular)/triangular_solve/custom-call.1 | solution.py:57
  84.2 9.8 %custom-call.35 = f32[2,1,64,64]{2,3,1,0:T(8,128)S(1)} custom-call(f32[2,1,64,64]{3,2,1,0:T(8,128)S(1)} %fusion.420), custom_call_target="InvertDiagBlocksLowerTriangular" | custom-call | tf_op jit(solution)/shard_map/jvp(vmap())/while/body/eval_jaxpr/jit(_solve_triangular)/triangular_solve/custom-call.1 | solution.py:57
  100.7 9.8 %custom-call.35 = f32[2,1,64,64]{2,3,1,0:T(8,128)S(1)} custom-call(f32[2,1,64,64]{3,2,1,0:T(8,128)S(1)} %fusion.420), custom_call_target="InvertDiagBlocksLowerTriangular" | custom-call | tf_op jit(solution)/shard_map/jvp(vmap())/while/body/eval_jaxpr/jit(_solve_triangular)/triangular_solve/custom-call.1 | solution.py:57
  128.2 45.1 %all-gather.9.cloned.1.call-done = f32[64,128,128]{2,1,0:T(8,128)} async-done(((f32[2,128,128]{2,1,0:T(8,128)}), f32[64,128,128]{2,1,0:T(8,128)}) %all-gather.9.cloned.1.call-update) | async-done | bytes 4194320 | tf_op jit(solution)/shard_map/all_gather | solution.py:24
  173.2 64.6 %all-gather.11.cloned.1.call-done = f32[64,128,128]{2,1,0:T(8,128)} async-done(((f32[2,128,128]{2,1,0:T(8,128)}), f32[64,128,128]{2,1,0:T(8,128)}) %all-gather.11.cloned.1.call-update) | async-done | bytes 4194320 | tf_op jit(solution)/shard_map/all_gather | solution.py:24
  237.9 80.1 %while.167 = (s32[]{:T(128)}, f32[2,128,128]{2,1,0:T(8,128)S(1)}, f32[2,128,128]{2,1,0:T(8,128)S(1)}, s32[]{:T(128)}, f32[32,2,128,128]{3,2,1,0:T(8,128)}, /*ind...) while((s32[]{:T(128)}, f32[2,128,128]{2,1,0:T(8,128)S(1)}, ...), condition=%wide.region_8.10_spmd.clone, body=%wide.region_7.9_spmd.clone.sunk | while | flops 100827144 | bytes 1706674 | solution.py:37
  318.0 47.8 %all-gather.15.cloned.1.call-done = f32[64,128,128]{2,1,0:T(8,128)} async-done(((f32[2,128,128]{2,1,0:T(8,128)}), f32[64,128,128]{2,1,0:T(8,128)}) %all-gather.15.cloned.1.call-update) | async-done | bytes 4194320 | tf_op jit(solution)/shard_map/all_gather | solution.py:24
  365.9 79.6 %while.168 = (s32[]{:T(128)}, f32[2,128,128]{2,1,0:T(8,128)S(1)}, f32[2,128,128]{2,1,0:T(8,128)S(1)}, s32[]{:T(128)}, f32[32,2,128,128]{3,2,1,0:T(8,128)}, /*ind...) while((s32[]{:T(128)}, f32[2,128,128]{2,1,0:T(8,128)S(1)}, f32[2,128,128]{2,1,0:T(8,128)S(1)}, ...), condition=%wide.region_10.12_spmd.clone, body=%wide.region_9.11_spmd.clone.sunk | while | flops 100827136 | bytes 1706612 | solution.py:37
  458.0 107.3 %while.164 = (s32[]{:T(128)}, f32[2,128,128]{2,1,0:T(8,128)S(1)}, f32[4,2,64,64]{3,2,1,0:T(8,128)}, f32[4,2,128,64]{2,3,1,0:T(8,128)}, f32[4,2,64,64]{3,2,1,0:T(...) while((s32[]{:T(128)}, f32[2,128,128]{2,1,0:T(8,128)S(1)}, ...), condition=%wide.region_13.15_spmd.clone.clone, body=%wide.region_11.14_spmd.clone.clone.sunk | while | flops 126194176 | bytes 3312057 | solution.py:86
  463.0 11.2 %custom-call.33 = f32[2,1,64,64]{2,3,1,0:T(8,128)} custom-call(f32[2,1,64,64]{3,2,1,0:T(8,128)} %select_bitcast_fusion.4), custom_call_target="InvertDiagBlocksLowerTriangular" | custom-call | tf_op jit(solution)/shard_map/jvp(vmap())/while/body/eval_jaxpr/jit(_solve_triangular)/triangular_solve/custom-call.1 | solution.py:57
  489.8 11.2 %custom-call.33 = f32[2,1,64,64]{2,3,1,0:T(8,128)} custom-call(f32[2,1,64,64]{3,2,1,0:T(8,128)} %select_bitcast_fusion.4), custom_call_target="InvertDiagBlocksLowerTriangular" | custom-call | tf_op jit(solution)/shard_map/jvp(vmap())/while/body/eval_jaxpr/jit(_solve_triangular)/triangular_solve/custom-call.1 | solution.py:57
  516.6 11.2 %custom-call.33 = f32[2,1,64,64]{2,3,1,0:T(8,128)} custom-call(f32[2,1,64,64]{3,2,1,0:T(8,128)} %select_bitcast_fusion.4), custom_call_target="InvertDiagBlocksLowerTriangular" | custom-call | tf_op jit(solution)/shard_map/jvp(vmap())/while/body/eval_jaxpr/jit(_solve_triangular)/triangular_solve/custom-call.1 | solution.py:57
  543.5 11.2 %custom-call.33 = f32[2,1,64,64]{2,3,1,0:T(8,128)} custom-call(f32[2,1,64,64]{3,2,1,0:T(8,128)} %select_bitcast_fusion.4), custom_call_target="InvertDiagBlocksLowerTriangular" | custom-call | tf_op jit(solution)/shard_map/jvp(vmap())/while/body/eval_jaxpr/jit(_solve_triangular)/triangular_solve/custom-call.1 | solution.py:57
  569.3 127.3 %while.165 = (s32[]{:T(128)}, f32[2,128,128]{2,1,0:T(8,128)S(1)}, f32[4,2,64,128]{3,2,1,0:T(8,128)}, f32[4,2,64,128]{3,2,1,0:T(8,128)}, f32[4,2,64,128]{3,2,0,1:...) while((s32[]{:T(128)}, f32[2,128,128]{2,1,0:T(8,128)S(1)}, ...), condition=%wide.region_25.27_spmd.clone.clone, body=%wide.region_14.26_spmd.clone.clone.sunk | while | flops 283857920 | bytes 5617773 | solution.py:86
  572.9 9.8 %custom-call.34 = f32[2,1,64,64]{2,3,1,0:T(8,128)S(1)} custom-call(f32[2,1,64,64]{3,2,1,0:T(8,128)S(1)} %select_bitcast_fusion.5), custom_call_target="InvertDiagBlocksLowerTriangular" | custom-call | tf_op jit(solution)/shard_map/transpose(jvp(vmap()))/while/body/eval_jaxpr/jit(_solve_triangular)/triangular_solve | solution.py:57
  604.8 9.8 %custom-call.34 = f32[2,1,64,64]{2,3,1,0:T(8,128)S(1)} custom-call(f32[2,1,64,64]{3,2,1,0:T(8,128)S(1)} %select_bitcast_fusion.5), custom_call_target="InvertDiagBlocksLowerTriangular" | custom-call | tf_op jit(solution)/shard_map/transpose(jvp(vmap()))/while/body/eval_jaxpr/jit(_solve_triangular)/triangular_solve | solution.py:57
  636.6 9.8 %custom-call.34 = f32[2,1,64,64]{2,3,1,0:T(8,128)S(1)} custom-call(f32[2,1,64,64]{3,2,1,0:T(8,128)S(1)} %select_bitcast_fusion.5), custom_call_target="InvertDiagBlocksLowerTriangular" | custom-call | tf_op jit(solution)/shard_map/transpose(jvp(vmap()))/while/body/eval_jaxpr/jit(_solve_triangular)/triangular_solve | solution.py:57
  668.4 9.8 %custom-call.34 = f32[2,1,64,64]{2,3,1,0:T(8,128)S(1)} custom-call(f32[2,1,64,64]{3,2,1,0:T(8,128)S(1)} %select_bitcast_fusion.5), custom_call_target="InvertDiagBlocksLowerTriangular" | custom-call | tf_op jit(solution)/shard_map/transpose(jvp(vmap()))/while/body/eval_jaxpr/jit(_solve_triangular)/triangular_solve | solution.py:57
  707.4 12.7 %all-to-all-start.1 = ((bf16[16,16,512]{2,1,0:T(8,128)(2,1)}), bf16[16,16,512]{2,1,0:T(8,128)(2,1)S(1)}, u32[]{:S(2)}, u32[]{:S(2)}) async-start(bf16[16,16,512]{2,1,0:T(8,128)(2,1)} %bitcast.32), calls=%async_computation.1 | async-start | bytes 524288 | tf_op jit(solution)/shard_map/all_to_all | solution.py:170
  720.8 66.5 %psum.7 = f32[4,512]{1,0:T(4,128)} all-reduce(f32[4,512]{1,0:T(4,128)S(1)} %pad_add_fusion.5), channel_id=1, replica_groups=mesh['ctx'=32,'head'=16] {'ctx'}, use_global_device_ids=true, to_apply=%region_34.36 | all-reduce | flops 2048 | bytes 16384 | tf_op jit(solution)/shard_map/psum | solution.py:173
  (748 shorter events, 393.9 us)
Async XLA Ops:
  7.2 438.4 %copy-start = (f32[2,128,128]{2,1,0:T(8,128)S(1)}, f32[2,128,128]{2,1,0:T(8,128)}, u32[]{:S(2)}) copy-start(f32[2,128,128]{2,1,0:T(8,128)} %param.25) | copy-start | bytes 393220
  8.9 33.1 %all-to-all-start = ((bf16[16,16,512]{2,0,1:T(8,128)(2,1)}), bf16[16,16,512]{2,0,1:T(8,128)(2,1)S(1)}, u32[]{:S(2)}, u32[]{:S(2)}) async-start(bf16[16,16,512]{2,0,1:T(8,128)(2,1)} %bitcast.435), calls=%async_computation | async-start | bytes 524288 | tf_op jit(solution)/shard_map/all_to_all | solution.py:138
  24.1 149.1 %all-gather.9.cloned.1.call-start = ((), (), s32[]{:S(2)}) async-start(), calls=%async_computation.2 | async-start | bytes 4325376 | tf_op jit(solution)/shard_map/all_gather | solution.py:24
  26.3 21.4 %copy-start.8 = (f32[1,512]{1,0:T(1,128)}, f32[1,512]{1,0:T(1,128)S(1)}, u32[]{:S(2)}) copy-start(f32[1,512]{1,0:T(1,128)S(1)} %get-tuple-element.3118) | copy-start | bytes 6148
  26.3 21.4 %copy-start.10 = (f32[1,512]{1,0:T(1,128)}, f32[1,512]{1,0:T(1,128)S(1)}, u32[]{:S(2)}) copy-start(f32[1,512]{1,0:T(1,128)S(1)} %get-tuple-element.3119) | copy-start | bytes 6148
  26.3 21.4 %copy-start.12 = (f32[1,512]{1,0:T(1,128)}, f32[1,512]{1,0:T(1,128)S(1)}, u32[]{:S(2)}) copy-start(f32[1,512]{1,0:T(1,128)S(1)} %get-tuple-element.3120) | copy-start | bytes 6148
  26.4 21.4 %copy-start.14 = (f32[1,512]{1,0:T(1,128)}, f32[1,512]{1,0:T(1,128)S(1)}, u32[]{:S(2)}) copy-start(f32[1,512]{1,0:T(1,128)S(1)} %get-tuple-element.3121) | copy-start | bytes 6148
  42.0 3.4 collective-permute-start
  48.5 66.4 %copy-start.5 = (bf16[256,256]{1,0:T(8,128)(2,1)S(1)}, bf16[256,256]{1,0:T(8,128)(2,1)}, u32[]{:S(2)}) copy-start(bf16[256,256]{1,0:T(8,128)(2,1)} %param.27) | copy-start | bytes 393220
  114.9 123.0 %all-gather.11.cloned.1.call-start = ((), (), s32[]{:S(2)}) async-start(), calls=%async_computation.3 | async-start | bytes 4325376 | tf_op jit(solution)/shard_map/all_gather | solution.py:24
  126.8 191.2 %all-gather.13.cloned.1.call-start = ((), (), s32[]{:S(2)}) async-start(), calls=%async_computation.4 | async-start | bytes 4325376 | tf_op jit(solution)/shard_map/all_gather | solution.py:24
  127.6 238.3 %all-gather.15.cloned.1.call-start = ((), (), s32[]{:S(2)}) async-start(), calls=%async_computation.5 | async-start | bytes 4325376 | tf_op jit(solution)/shard_map/all_gather | solution.py:24
  318.0 47.9 %copy-start.4 = (f32[2,128,128]{2,1,0:T(8,128)}, f32[2,128,128]{2,1,0:T(8,128)S(1)}, u32[]{:S(2)}) copy-start(f32[2,128,128]{2,1,0:T(8,128)S(1)} %get-tuple-element.2004) | copy-start | bytes 393220
  569.3 29.8 %copy-start.7 = (f32[4,2,64]{2,1,0:T(2,128)S(1)}, f32[4,2,64]{2,1,0:T(2,128)}, u32[]{:S(2)}) copy-start(f32[4,2,64]{2,1,0:T(2,128)} %get-tuple-element.4201) | copy-start | bytes 6148 | tf_op jit(solution)/shard_map/transpose(jvp(vmap()))/while
  569.3 30.1 %copy-start.6 = (f32[4,2,64]{2,1,0:T(2,128)S(1)}, f32[4,2,64]{2,1,0:T(2,128)}, u32[]{:S(2)}) copy-start(f32[4,2,64]{2,1,0:T(2,128)} %get-tuple-element.4198) | copy-start | bytes 6148 | tf_op jit(solution)/shard_map/transpose(jvp(vmap()))/while
  601.2 29.8 %copy-start.7 = (f32[4,2,64]{2,1,0:T(2,128)S(1)}, f32[4,2,64]{2,1,0:T(2,128)}, u32[]{:S(2)}) copy-start(f32[4,2,64]{2,1,0:T(2,128)} %get-tuple-element.4201) | copy-start | bytes 6148 | tf_op jit(solution)/shard_map/transpose(jvp(vmap()))/while
  601.2 30.0 %copy-start.6 = (f32[4,2,64]{2,1,0:T(2,128)S(1)}, f32[4,2,64]{2,1,0:T(2,128)}, u32[]{:S(2)}) copy-start(f32[4,2,64]{2,1,0:T(2,128)} %get-tuple-element.4198) | copy-start | bytes 6148 | tf_op jit(solution)/shard_map/transpose(jvp(vmap()))/while
  633.0 29.8 %copy-start.7 = (f32[4,2,64]{2,1,0:T(2,128)S(1)}, f32[4,2,64]{2,1,0:T(2,128)}, u32[]{:S(2)}) copy-start(f32[4,2,64]{2,1,0:T(2,128)} %get-tuple-element.4201) | copy-start | bytes 6148 | tf_op jit(solution)/shard_map/transpose(jvp(vmap()))/while
  633.0 30.0 %copy-start.6 = (f32[4,2,64]{2,1,0:T(2,128)S(1)}, f32[4,2,64]{2,1,0:T(2,128)}, u32[]{:S(2)}) copy-start(f32[4,2,64]{2,1,0:T(2,128)} %get-tuple-element.4198) | copy-start | bytes 6148 | tf_op jit(solution)/shard_map/transpose(jvp(vmap()))/while
  664.8 29.8 %copy-start.7 = (f32[4,2,64]{2,1,0:T(2,128)S(1)}, f32[4,2,64]{2,1,0:T(2,128)}, u32[]{:S(2)}) copy-start(f32[4,2,64]{2,1,0:T(2,128)} %get-tuple-element.4201) | copy-start | bytes 6148 | tf_op jit(solution)/shard_map/transpose(jvp(vmap()))/while
  664.8 30.1 %copy-start.6 = (f32[4,2,64]{2,1,0:T(2,128)S(1)}, f32[4,2,64]{2,1,0:T(2,128)}, u32[]{:S(2)}) copy-start(f32[4,2,64]{2,1,0:T(2,128)} %get-tuple-element.4198) | copy-start | bytes 6148 | tf_op jit(solution)/shard_map/transpose(jvp(vmap()))/while
  703.5 83.7 %copy-start.20 = (f32[2,256]{1,0:T(2,128)S(1)}, f32[2,256]{1,0:T(2,128)}, u32[]{:S(2)}) copy-start(f32[2,256]{1,0:T(2,128)} %param.23) | copy-start | bytes 6148
  703.6 3.1 collective-permute-start.1
  707.4 80.5 %all-to-all-start.1 = ((bf16[16,16,512]{2,1,0:T(8,128)(2,1)}), bf16[16,16,512]{2,1,0:T(8,128)(2,1)S(1)}, u32[]{:S(2)}, u32[]{:S(2)}) async-start(bf16[16,16,512]{2,1,0:T(8,128)(2,1)} %bitcast.32), calls=%async_computation.1 | async-start | bytes 524288 | tf_op jit(solution)/shard_map/all_to_all | solution.py:170
  (11 other events, 52.7 us)
Sparse Core Ops, SparseCore 0:
  115.0 58.1 all-gather.8
  176.9 60.8 all-gather.10
  241.0 60.9 all-gather.12
  304.9 60.8 all-gather.14
where the time goes:
time: 802 us; the launch traced here: 795 us
  matrix products  258 us (32%)
  other arithmetic  180 us (22%)
  waiting for transfers between devices  176 us (22%)
  blocking collectives  66.5 us (8%)
  local copies, waits for them, and re-layouts  64.8 us (8%)
  starting transfers between devices  30.8 us (4%)
  between operations  14.3 us (2%)
    all_gather x4, waiting for transfers between devices, prefix(): everything = jax.tree.map(lambda part: lax.all_gather(part, axis), value)  158 us
    another operation x32, other arithmetic, block_step(): solved = jax.scipy.linalg.solve_triangular(system, right_sides, lower=True)  133 us
    dot_general x64, matrix products, compose(): jnp.einsum('hij,hjk->hik', later[0], earlier[1], precision=highest)  79.3 us
    dot_general x64, matrix products, compose(): matrix = jnp.einsum('hij,hjk->hik', later[0], earlier[0], precision=highest)  75.2 us
    psum x1, blocking collectives, on_device(): weight_total = lax.psum(grad_weight, 'ctx')  66.5 us
    dynamic_update_slice x24, other arithmetic, run_head(): (state_end, transit), outputs = lax.scan(block_step, start, pieces)  18.8 us
    dot_general x16, matrix products, block_step(): scores = ratios * jnp.dot(queries, key_feats.T, precision=highest)  18.5 us
    dot_general x20, matrix products, block_step(): jnp.dot(tail_keys.T, update, precision=highest)  17.8 us
  transfers between devices with their start and end apart: 8, of which 5 were waited for; matrix products, arithmetic and copies ran while one was open for 12% of the time, Pallas kernels for 0%

commit v1 on v0

--- a/solution.py
+++ b/solution.py
@@ -135,7 +135,10 @@
     final_state_grad,
     grad_out,
 ):
-    local_in = lax.all_to_all(mixed_in, "head", split_axis=1, concat_axis=0, tiled=True)
+    local_in = jnp.concatenate(
+        lax.all_to_all(jnp.stack(jnp.split(mixed_in, lax.axis_size("head"), axis=1)), "head", 0, 0),
+        axis=0,
+    )
     edge_rows = from_behind(local_in[-(KW - 1) :], "ctx", 1)
     extended = jnp.concatenate([edge_rows, local_in], axis=0).astype(jnp.float32)
     cotangent = grad_out.astype(jnp.float32)

time: 802 us -> 819 us (1.021)
  local copies, waits for them, and re-layouts: 64.8 us -> 85.1 us
    unnamed x42 -> x55, local copies, waits for them, and re-layouts: 2.93 us -> 24.4 us
where the time goes in v1:
time: 819 us; the launch traced here: 812 us
  matrix products  255 us (31%)
  other arithmetic  178 us (22%)
  waiting for transfers between devices  177 us (22%)
  local copies, waits for them, and re-layouts  85.1 us (10%)
  blocking collectives  66.4 us (8%)
  starting transfers between devices  30.8 us (4%)
  between operations  14.4 us (2%)
    all_gather x4, waiting for transfers between devices, prefix(): everything = jax.tree.map(lambda part: lax.all_gather(part, axis), value)  158 us
    another operation x32, other arithmetic, block_step(): solved = jax.scipy.linalg.solve_triangular(system, right_sides, lower=True)  133 us
    dot_general x64, matrix products, compose(): jnp.einsum('hij,hjk->hik', later[0], earlier[1], precision=highest)  79.3 us
    dot_general x64, matrix products, compose(): matrix = jnp.einsum('hij,hjk->hik', later[0], earlier[0], precision=highest)  75.3 us
    psum x1, blocking collectives, on_device(): weight_total = lax.psum(grad_weight, 'ctx')  66.4 us
    unnamed x55, local copies, waits for them, and re-layouts  24.4 us
    dot_general x16, matrix products, block_step(): scores = ratios * jnp.dot(queries, key_feats.T, precision=highest)  18.5 us
  transfers between devices with their start and end apart: 8, of which 5 were waited for; matrix products, arithmetic and copies ran while one was open for 12% of the time, Pallas kernels for 0%

profile of v1, /device:TPU:32, one launch (start us, length us, event | category | flops | bytes accessed | tf_op | source)
XLA Modules:
  0.0 811.5 jit_solution(10520390269512810290)
XLA Ops:
  28.4 15.2 %all-to-all-start = ((bf16[16,16,512]{2,1,0:T(8,128)(2,1)}), bf16[16,16,512]{2,1,0:T(8,128)(2,1)S(1)}, u32[]{:S(2)}, u32[]{:S(2)}) async-start(bf16[16,16,512]{2,1,0:T(8,128)(2,1)} %constant_dynamic-update-slice_fusion.11), calls=%async_computation | async-start | bytes 524288 | tf_op jit(solution)/shard_map/all_to_all | solution.py:139
  45.9 15.6 %all-to-all-done = bf16[16,16,512]{2,1,0:T(8,128)(2,1)S(1)} async-done(((bf16[16,16,512]{2,1,0:T(8,128)(2,1)}), bf16[16,16,512]{2,1,0:T(8,128)(2,1)S(1)}, u32[]{:S(2)}, u32[]{:S(2)}) %all-to-all-start) | async-done | bytes 262176 | tf_op jit(solution)/shard_map/all_to_all | solution.py:139
  67.4 63.1 %while.169 = (s32[]{:T(128)}, f32[2,128,128]{2,1,0:T(8,128)S(1)}, f32[2,128,128]{2,1,0:T(8,128)S(1)}, f32[4,2,64,128]{3,2,1,0:T(8,128)S(1)}, f32[4,2,64,1]{2,1,3...) while((s32[]{:T(128)}, f32[2,128,128]{2,1,0:T(8,128)S(1)}, ...), condition=%wide.region_4.6_spmd.clone.clone, body=%wide.region_2.5_spmd.clone.clone.sunk | while | flops 176640128 | bytes 2981140 | solution.py:86
  70.4 9.8 %custom-call.37 = f32[2,1,64,64]{2,3,1,0:T(8,128)S(1)} custom-call(f32[2,1,64,64]{3,2,1,0:T(8,128)S(1)} %fusion.420), custom_call_target="InvertDiagBlocksLowerTriangular" | custom-call | tf_op jit(solution)/shard_map/jvp(vmap())/while/body/eval_jaxpr/jit(_solve_triangular)/triangular_solve/custom-call.1 | solution.py:57
  86.1 9.8 %custom-call.37 = f32[2,1,64,64]{2,3,1,0:T(8,128)S(1)} custom-call(f32[2,1,64,64]{3,2,1,0:T(8,128)S(1)} %fusion.420), custom_call_target="InvertDiagBlocksLowerTriangular" | custom-call | tf_op jit(solution)/shard_map/jvp(vmap())/while/body/eval_jaxpr/jit(_solve_triangular)/triangular_solve/custom-call.1 | solution.py:57
  101.9 9.8 %custom-call.37 = f32[2,1,64,64]{2,3,1,0:T(8,128)S(1)} custom-call(f32[2,1,64,64]{3,2,1,0:T(8,128)S(1)} %fusion.420), custom_call_target="InvertDiagBlocksLowerTriangular" | custom-call | tf_op jit(solution)/shard_map/jvp(vmap())/while/body/eval_jaxpr/jit(_solve_triangular)/triangular_solve/custom-call.1 | solution.py:57
  117.7 9.8 %custom-call.37 = f32[2,1,64,64]{2,3,1,0:T(8,128)S(1)} custom-call(f32[2,1,64,64]{3,2,1,0:T(8,128)S(1)} %fusion.420), custom_call_target="InvertDiagBlocksLowerTriangular" | custom-call | tf_op jit(solution)/shard_map/jvp(vmap())/while/body/eval_jaxpr/jit(_solve_triangular)/triangular_solve/custom-call.1 | solution.py:57
  143.7 46.0 %all-gather.9.cloned.1.call-done = f32[64,128,128]{2,1,0:T(8,128)} async-done(((f32[2,128,128]{2,1,0:T(8,128)}), f32[64,128,128]{2,1,0:T(8,128)}) %all-gather.9.cloned.1.call-update) | async-done | bytes 4194320 | tf_op jit(solution)/shard_map/all_gather | solution.py:24
  189.7 64.6 %all-gather.11.cloned.1.call-done = f32[64,128,128]{2,1,0:T(8,128)} async-done(((f32[2,128,128]{2,1,0:T(8,128)}), f32[64,128,128]{2,1,0:T(8,128)}) %all-gather.11.cloned.1.call-update) | async-done | bytes 4194320 | tf_op jit(solution)/shard_map/all_gather | solution.py:24
  254.3 80.1 %while.167 = (s32[]{:T(128)}, f32[2,128,128]{2,1,0:T(8,128)S(1)}, f32[2,128,128]{2,1,0:T(8,128)S(1)}, s32[]{:T(128)}, f32[32,2,128,128]{3,2,1,0:T(8,128)}, /*ind...) while((s32[]{:T(128)}, f32[2,128,128]{2,1,0:T(8,128)S(1)}, ...), condition=%wide.region_8.10_spmd.clone, body=%wide.region_7.9_spmd.clone.sunk | while | flops 100827144 | bytes 1706674 | solution.py:37
  334.5 47.8 %all-gather.15.cloned.1.call-done = f32[64,128,128]{2,1,0:T(8,128)} async-done(((f32[2,128,128]{2,1,0:T(8,128)}), f32[64,128,128]{2,1,0:T(8,128)}) %all-gather.15.cloned.1.call-update) | async-done | bytes 4194320 | tf_op jit(solution)/shard_map/all_gather | solution.py:24
  382.4 79.7 %while.168 = (s32[]{:T(128)}, f32[2,128,128]{2,1,0:T(8,128)S(1)}, f32[2,128,128]{2,1,0:T(8,128)S(1)}, s32[]{:T(128)}, f32[32,2,128,128]{3,2,1,0:T(8,128)}, /*ind...) while((s32[]{:T(128)}, f32[2,128,128]{2,1,0:T(8,128)S(1)}, f32[2,128,128]{2,1,0:T(8,128)S(1)}, ...), condition=%wide.region_10.12_spmd.clone, body=%wide.region_9.11_spmd.clone.sunk | while | flops 100827136 | bytes 1706612 | solution.py:37
  474.5 107.3 %while.164 = (s32[]{:T(128)}, f32[2,128,128]{2,1,0:T(8,128)S(1)}, f32[4,2,64,64]{3,2,1,0:T(8,128)}, f32[4,2,128,64]{2,3,1,0:T(8,128)}, f32[4,2,64,64]{3,2,1,0:T(...) while((s32[]{:T(128)}, f32[2,128,128]{2,1,0:T(8,128)S(1)}, ...), condition=%wide.region_13.15_spmd.clone.clone, body=%wide.region_11.14_spmd.clone.clone.sunk | while | flops 126194176 | bytes 3312057 | solution.py:86
  479.6 11.2 %custom-call.35 = f32[2,1,64,64]{2,3,1,0:T(8,128)} custom-call(f32[2,1,64,64]{3,2,1,0:T(8,128)} %select_bitcast_fusion.4), custom_call_target="InvertDiagBlocksLowerTriangular" | custom-call | tf_op jit(solution)/shard_map/jvp(vmap())/while/body/eval_jaxpr/jit(_solve_triangular)/triangular_solve/custom-call.1 | solution.py:57
  506.4 11.2 %custom-call.35 = f32[2,1,64,64]{2,3,1,0:T(8,128)} custom-call(f32[2,1,64,64]{3,2,1,0:T(8,128)} %select_bitcast_fusion.4), custom_call_target="InvertDiagBlocksLowerTriangular" | custom-call | tf_op jit(solution)/shard_map/jvp(vmap())/while/body/eval_jaxpr/jit(_solve_triangular)/triangular_solve/custom-call.1 | solution.py:57
  533.2 11.2 %custom-call.35 = f32[2,1,64,64]{2,3,1,0:T(8,128)} custom-call(f32[2,1,64,64]{3,2,1,0:T(8,128)} %select_bitcast_fusion.4), custom_call_target="InvertDiagBlocksLowerTriangular" | custom-call | tf_op jit(solution)/shard_map/jvp(vmap())/while/body/eval_jaxpr/jit(_solve_triangular)/triangular_solve/custom-call.1 | solution.py:57
  560.0 11.2 %custom-call.35 = f32[2,1,64,64]{2,3,1,0:T(8,128)} custom-call(f32[2,1,64,64]{3,2,1,0:T(8,128)} %select_bitcast_fusion.4), custom_call_target="InvertDiagBlocksLowerTriangular" | custom-call | tf_op jit(solution)/shard_map/jvp(vmap())/while/body/eval_jaxpr/jit(_solve_triangular)/triangular_solve/custom-call.1 | solution.py:57
  585.9 127.4 %while.165 = (s32[]{:T(128)}, f32[2,128,128]{2,1,0:T(8,128)S(1)}, f32[4,2,64,128]{3,2,1,0:T(8,128)}, f32[4,2,64,128]{3,2,1,0:T(8,128)}, f32[4,2,64,128]{3,2,0,1:...) while((s32[]{:T(128)}, f32[2,128,128]{2,1,0:T(8,128)S(1)}, ...), condition=%wide.region_25.27_spmd.clone.clone, body=%wide.region_14.26_spmd.clone.clone.sunk | while | flops 283857920 | bytes 5617773 | solution.py:86
  589.5 9.8 %custom-call.36 = f32[2,1,64,64]{2,3,1,0:T(8,128)S(1)} custom-call(f32[2,1,64,64]{3,2,1,0:T(8,128)S(1)} %select_bitcast_fusion.5), custom_call_target="InvertDiagBlocksLowerTriangular" | custom-call | tf_op jit(solution)/shard_map/transpose(jvp(vmap()))/while/body/eval_jaxpr/jit(_solve_triangular)/triangular_solve | solution.py:57
  621.3 9.8 %custom-call.36 = f32[2,1,64,64]{2,3,1,0:T(8,128)S(1)} custom-call(f32[2,1,64,64]{3,2,1,0:T(8,128)S(1)} %select_bitcast_fusion.5), custom_call_target="InvertDiagBlocksLowerTriangular" | custom-call | tf_op jit(solution)/shard_map/transpose(jvp(vmap()))/while/body/eval_jaxpr/jit(_solve_triangular)/triangular_solve | solution.py:57
  653.2 9.8 %custom-call.36 = f32[2,1,64,64]{2,3,1,0:T(8,128)S(1)} custom-call(f32[2,1,64,64]{3,2,1,0:T(8,128)S(1)} %select_bitcast_fusion.5), custom_call_target="InvertDiagBlocksLowerTriangular" | custom-call | tf_op jit(solution)/shard_map/transpose(jvp(vmap()))/while/body/eval_jaxpr/jit(_solve_triangular)/triangular_solve | solution.py:57
  685.0 9.8 %custom-call.36 = f32[2,1,64,64]{2,3,1,0:T(8,128)S(1)} custom-call(f32[2,1,64,64]{3,2,1,0:T(8,128)S(1)} %select_bitcast_fusion.5), custom_call_target="InvertDiagBlocksLowerTriangular" | custom-call | tf_op jit(solution)/shard_map/transpose(jvp(vmap()))/while/body/eval_jaxpr/jit(_solve_triangular)/triangular_solve | solution.py:57
  723.8 12.7 %all-to-all-start.1 = ((bf16[16,16,512]{2,1,0:T(8,128)(2,1)}), bf16[16,16,512]{2,1,0:T(8,128)(2,1)S(1)}, u32[]{:S(2)}, u32[]{:S(2)}) async-start(bf16[16,16,512]{2,1,0:T(8,128)(2,1)} %bitcast.48), calls=%async_computation.1 | async-start | bytes 524288 | tf_op jit(solution)/shard_map/all_to_all | solution.py:173
  737.2 66.4 %psum.7 = f32[4,512]{1,0:T(4,128)} all-reduce(f32[4,512]{1,0:T(4,128)S(1)} %pad_add_fusion.5), channel_id=1, replica_groups=mesh['ctx'=32,'head'=16] {'ctx'}, use_global_device_ids=true, to_apply=%region_34.36 | all-reduce | flops 2048 | bytes 16384 | tf_op jit(solution)/shard_map/psum | solution.py:176
  (761 shorter events, 405.9 us)
Async XLA Ops:
  7.2 454.9 %copy-start = (f32[2,128,128]{2,1,0:T(8,128)S(1)}, f32[2,128,128]{2,1,0:T(8,128)}, u32[]{:S(2)}) copy-start(f32[2,128,128]{2,1,0:T(8,128)} %param.25) | copy-start | bytes 393220
  28.4 33.1 %all-to-all-start = ((bf16[16,16,512]{2,1,0:T(8,128)(2,1)}), bf16[16,16,512]{2,1,0:T(8,128)(2,1)S(1)}, u32[]{:S(2)}, u32[]{:S(2)}) async-start(bf16[16,16,512]{2,1,0:T(8,128)(2,1)} %constant_dynamic-update-slice_fusion.11), calls=%async_computation | async-start | bytes 524288 | tf_op jit(solution)/shard_map/all_to_all | solution.py:139
  43.6 146.1 %all-gather.9.cloned.1.call-start = ((), (), s32[]{:S(2)}) async-start(), calls=%async_computation.2 | async-start | bytes 4325376 | tf_op jit(solution)/shard_map/all_gather | solution.py:24
  45.8 21.5 %copy-start.7 = (f32[1,512]{1,0:T(1,128)}, f32[1,512]{1,0:T(1,128)S(1)}, u32[]{:S(2)}) copy-start(f32[1,512]{1,0:T(1,128)S(1)} %get-tuple-element.3216) | copy-start | bytes 6148
  45.8 21.5 %copy-start.9 = (f32[1,512]{1,0:T(1,128)}, f32[1,512]{1,0:T(1,128)S(1)}, u32[]{:S(2)}) copy-start(f32[1,512]{1,0:T(1,128)S(1)} %get-tuple-element.3217) | copy-start | bytes 6148
  45.8 21.5 %copy-start.11 = (f32[1,512]{1,0:T(1,128)}, f32[1,512]{1,0:T(1,128)S(1)}, u32[]{:S(2)}) copy-start(f32[1,512]{1,0:T(1,128)S(1)} %get-tuple-element.3218) | copy-start | bytes 6148
  45.8 21.5 %copy-start.13 = (f32[1,512]{1,0:T(1,128)}, f32[1,512]{1,0:T(1,128)S(1)}, u32[]{:S(2)}) copy-start(f32[1,512]{1,0:T(1,128)S(1)} %get-tuple-element.3219) | copy-start | bytes 6148
  61.5 3.4 collective-permute-start
  131.3 123.0 %all-gather.11.cloned.1.call-start = ((), (), s32[]{:S(2)}) async-start(), calls=%async_computation.3 | async-start | bytes 4325376 | tf_op jit(solution)/shard_map/all_gather | solution.py:24
  142.4 192.1 %all-gather.13.cloned.1.call-start = ((), (), s32[]{:S(2)}) async-start(), calls=%async_computation.4 | async-start | bytes 4325376 | tf_op jit(solution)/shard_map/all_gather | solution.py:24
  143.1 239.2 %all-gather.15.cloned.1.call-start = ((), (), s32[]{:S(2)}) async-start(), calls=%async_computation.5 | async-start | bytes 4325376 | tf_op jit(solution)/shard_map/all_gather | solution.py:24
  334.5 47.9 %copy-start.4 = (f32[2,128,128]{2,1,0:T(8,128)}, f32[2,128,128]{2,1,0:T(8,128)S(1)}, u32[]{:S(2)}) copy-start(f32[2,128,128]{2,1,0:T(8,128)S(1)} %get-tuple-element.2004) | copy-start | bytes 393220
  585.9 29.8 %copy-start.6 = (f32[4,2,64]{2,1,0:T(2,128)S(1)}, f32[4,2,64]{2,1,0:T(2,128)}, u32[]{:S(2)}) copy-start(f32[4,2,64]{2,1,0:T(2,128)} %get-tuple-element.4299) | copy-start | bytes 6148 | tf_op jit(solution)/shard_map/transpose(jvp(vmap()))/while
  585.9 30.1 %copy-start.5 = (f32[4,2,64]{2,1,0:T(2,128)S(1)}, f32[4,2,64]{2,1,0:T(2,128)}, u32[]{:S(2)}) copy-start(f32[4,2,64]{2,1,0:T(2,128)} %get-tuple-element.4296) | copy-start | bytes 6148 | tf_op jit(solution)/shard_map/transpose(jvp(vmap()))/while
  617.7 29.8 %copy-start.6 = (f32[4,2,64]{2,1,0:T(2,128)S(1)}, f32[4,2,64]{2,1,0:T(2,128)}, u32[]{:S(2)}) copy-start(f32[4,2,64]{2,1,0:T(2,128)} %get-tuple-element.4299) | copy-start | bytes 6148 | tf_op jit(solution)/shard_map/transpose(jvp(vmap()))/while
  617.7 30.0 %copy-start.5 = (f32[4,2,64]{2,1,0:T(2,128)S(1)}, f32[4,2,64]{2,1,0:T(2,128)}, u32[]{:S(2)}) copy-start(f32[4,2,64]{2,1,0:T(2,128)} %get-tuple-element.4296) | copy-start | bytes 6148 | tf_op jit(solution)/shard_map/transpose(jvp(vmap()))/while
  649.6 29.8 %copy-start.6 = (f32[4,2,64]{2,1,0:T(2,128)S(1)}, f32[4,2,64]{2,1,0:T(2,128)}, u32[]{:S(2)}) copy-start(f32[4,2,64]{2,1,0:T(2,128)} %get-tuple-element.4299) | copy-start | bytes 6148 | tf_op jit(solution)/shard_map/transpose(jvp(vmap()))/while
  649.6 30.0 %copy-start.5 = (f32[4,2,64]{2,1,0:T(2,128)S(1)}, f32[4,2,64]{2,1,0:T(2,128)}, u32[]{:S(2)}) copy-start(f32[4,2,64]{2,1,0:T(2,128)} %get-tuple-element.4296) | copy-start | bytes 6148 | tf_op jit(solution)/shard_map/transpose(jvp(vmap()))/while
  681.4 29.8 %copy-start.6 = (f32[4,2,64]{2,1,0:T(2,128)S(1)}, f32[4,2,64]{2,1,0:T(2,128)}, u32[]{:S(2)}) copy-start(f32[4,2,64]{2,1,0:T(2,128)} %get-tuple-element.4299) | copy-start | bytes 6148 | tf_op jit(solution)/shard_map/transpose(jvp(vmap()))/while
  681.4 30.1 %copy-start.5 = (f32[4,2,64]{2,1,0:T(2,128)S(1)}, f32[4,2,64]{2,1,0:T(2,128)}, u32[]{:S(2)}) copy-start(f32[4,2,64]{2,1,0:T(2,128)} %get-tuple-element.4296) | copy-start | bytes 6148 | tf_op jit(solution)/shard_map/transpose(jvp(vmap()))/while
  719.9 16.6 %copy-start.15 = (f32[4,2,64]{2,1,0:T(2,128)S(1)}, f32[4,2,64]{2,1,0:T(2,128)}, u32[]{:S(2)}) copy-start(f32[4,2,64]{2,1,0:T(2,128)} %get-tuple-element.2034) | copy-start | bytes 6148
  720.0 83.7 %copy-start.19 = (f32[2,256]{1,0:T(2,128)S(1)}, f32[2,256]{1,0:T(2,128)}, u32[]{:S(2)}) copy-start(f32[2,256]{1,0:T(2,128)} %param.23) | copy-start | bytes 6148
  720.0 3.1 collective-permute-start.1
  723.8 80.5 %all-to-all-start.1 = ((bf16[16,16,512]{2,1,0:T(8,128)(2,1)}), bf16[16,16,512]{2,1,0:T(8,128)(2,1)S(1)}, u32[]{:S(2)}, u32[]{:S(2)}) async-start(bf16[16,16,512]{2,1,0:T(8,128)(2,1)} %bitcast.48), calls=%async_computation.1 | async-start | bytes 524288 | tf_op jit(solution)/shard_map/all_to_all | solution.py:173
  (10 other events, 39.2 us)
Sparse Core Ops, SparseCore 0:
  131.5 58.1 all-gather.8
  193.4 60.8 all-gather.10
  257.4 60.9 all-gather.12
  321.4 60.8 all-gather.14
